TPU v7x, 512 devices: a whole 4x8x8 slice. The times are simulated.
512 devices in a mesh: fsdp: 32 (over z_hi, x, core), seq: 16 (over z_lo, y).
Axes of the slice: x: 4, y: 8, z: 8 (z_hi: 4, z_lo: 2; z = z_hi * 2 + z_lo), core: 2. Of those that a mesh axis runs over, the one named last changes fastest.
Arguments:
- video_qkv: bfloat16 [32, 2048, 3, 4096], P('fsdp', 'seq'), may hold values from -6 to 6
- reference_rows: bfloat16 [32, 64, 5120], P('fsdp', 'seq'), may hold values from -150 to 150
- kv_weight: bfloat16 [5120, 2, 4096], P('fsdp', None, 'seq'), may hold values from -0.125 to 0.125
- pose_table: bfloat16 [256, 4096], P('fsdp', 'seq'), may hold values from -6 to 6
- pose_ids: int32 [32, 2048], P('fsdp', 'seq'), may hold values from 0 to 255
- frame_counts: int32 [32], P('fsdp'), may hold values from 1 to 4, as said below
Outputs:
- attended: bfloat16 [32, 2048, 4096], P('fsdp', 'seq')
Inputs may be any that keep to these rules, and one draw needn't show every extreme that they name: `frame_counts`: every clip has 1 to 4 reference frames in the window, each making 16 slots live; in every draw some clip has exactly 4 and another exactly 1.
All inputs are finite; a program needn't handle non-finite values.
Results may differ from a plain program's by a relative error of at most 0.011.
Values may be sent and summed in bfloat16 or wider, within the bound.
No kernel may reach another device: no remote copies, remote signals or barrier semaphores. Data moves between devices by JAX's collectives and lax.ppermute only.
A program may use at most 64 MiB of HBM per device.

v0:
```python
import math
import jax
import jax.numpy as jnp
from jax import lax
from jax.sharding import PartitionSpec as P

HD = 128
TPF = 16
POSE = 256


def layer_norm(row_block):
    row_mean = jnp.mean(row_block, axis=-1, keepdims=True)
    centered = row_block - row_mean
    row_var = jnp.mean(centered * centered, axis=-1, keepdims=True)
    return centered * lax.rsqrt(row_var + 1e-06)


def pose_lookup(token_ids, codebook):
    onehot = (token_ids[:, None] == jnp.arange(POSE, dtype=jnp.int32)[None, :]).astype(jnp.bfloat16)
    return jnp.dot(onehot, codebook, preferred_element_type=jnp.float32)


def shards(video_qkv, reference_rows, kv_weight, pose_table, pose_ids, frame_counts):
    score_scale = 1.0 / math.sqrt(HD)
    query_part = video_qkv[:, :, 0:1, :]
    pair_part = video_qkv[:, :, 1:3, :]
    codebook_cols = lax.all_gather(pose_table, "seq", axis=1, tiled=True)
    codebook = lax.all_gather(codebook_cols, "fsdp", axis=0, tiled=True)
    lookup = pose_lookup(pose_ids[0], codebook)
    query_part = (query_part.astype(jnp.float32) + lookup[None, :, None, :]).astype(jnp.bfloat16)
    query_heads, pair_heads = (
        lax.all_to_all(query_part, "seq", split_axis=3, concat_axis=1, tiled=True),
        lax.all_to_all(pair_part, "seq", split_axis=3, concat_axis=1, tiled=True),
    )
    normed = layer_norm(reference_rows[0].astype(jnp.float32)).astype(jnp.bfloat16)
    all_rows = lax.all_gather(normed, "seq", axis=0, tiled=True)
    ref_count = all_rows.shape[0]
    head_width = kv_weight.shape[2]
    piece = lax.all_gather(kv_weight, "fsdp", axis=0, tiled=True)
    kv_sum = jnp.dot(
        all_rows, piece.reshape(piece.shape[0], 2 * head_width), preferred_element_type=jnp.float32
    )
    ref_kv = kv_sum.astype(jnp.bfloat16).reshape(ref_count, 2, head_width)
    video_len = query_heads.shape[1]
    heads_here = head_width // HD
    key_total = video_len + ref_count
    key_rows = jnp.concatenate([pair_heads[0, :, 0, :], ref_kv[:, 0, :]], axis=0).reshape(
        key_total, heads_here, HD
    )
    value_rows = jnp.concatenate([pair_heads[0, :, 1, :], ref_kv[:, 1, :]], axis=0).reshape(
        key_total, heads_here, HD
    )
    live_keys = jnp.arange(key_total, dtype=jnp.int32) < video_len + TPF * frame_counts[0]
    block_rows = min(512, video_len)
    block_count = video_len // block_rows

    def attend(query_block):
        scores = (
            jnp.einsum("bhd,khd->hbk", query_block, key_rows, preferred_element_type=jnp.float32)
            * score_scale
        )
        scores = jnp.where(live_keys[None, None, :], scores, -1e30)
        row_max = jnp.max(scores, axis=-1, keepdims=True)
        expo = jnp.where(live_keys[None, None, :], jnp.exp(scores - row_max), 0.0)
        row_total = jnp.sum(expo, axis=-1, keepdims=True)
        weights = (expo / row_total).astype(jnp.bfloat16)
        mixed = jnp.einsum("hbk,khd->bhd", weights, value_rows, preferred_element_type=jnp.float32)
        return mixed.astype(jnp.bfloat16)

    query_blocks = query_heads.reshape(block_count, block_rows, heads_here, HD)
    attended = lax.map(attend, query_blocks).reshape(1, video_len, head_width)
    return lax.all_to_all(attended, "seq", split_axis=1, concat_axis=2, tiled=True)


def solution(mesh):
    placed = (
        P("fsdp", "seq", None, None),
        P("fsdp", "seq", None),
        P("fsdp", None, "seq"),
        P("fsdp", "seq"),
        P("fsdp", "seq"),
        P("fsdp"),
    )
    return jax.shard_map(
        shards, mesh=mesh, in_specs=placed, out_specs=P("fsdp", "seq", None), check_vma=False
    )
```

profile of v0, /device:TPU:4, one launch (start us, length us, event | category | flops | bytes accessed | tf_op | source)
XLA Modules:
  0.0 340.3 jit_solution(14495082860246076433)
XLA Ops:
  6.5 37.7 %all_gather.12 = bf16[8,4096]{1,0:T(8,128)(2,1)} all-gather(bf16[8,256]{1,0:T(8,128)(2,1)} %param.11), channel_id=1, replica_groups=mesh['fsdp'=32,'seq'=16] {'seq'}, dimensions={1}, use_global_device_ids=true | all-gather | bytes 69632 | tf_op jit(solution)/shard_map/all_gather | solution.py:28
  45.0 1.6 slice-done
  46.6 3.8 %copy.76 = bf16[1,128,2,4096]{1,2,0,3:T(2,128)(2,1)} copy(bf16[1,128,2,4096]{3,1,2,0:T(8,128)(2,1)S(1)} %slice-done) | data formatting | bytes 4194304
  50.3 3.8 %all-to-all-start.1 = ((bf16[1,128,2,4096]{1,2,0,3:T(2,128)(2,1)}), bf16[1,128,2,4096]{1,2,0,3:T(2,128)(2,1)S(1)}, u32[]{:S(2)}, u32[]{:S(2)}) async-start(bf16[1,128,2,4096]{1,2,0,3:T(2,128)(2,1)} %copy.76), calls=%async_computation.1 | async-start | bytes 4194304 | tf_op jit(solution)/shard_map/all_to_all | solution.py:34
  54.6 53.1 %all-gather.4.cloned.1.call-done = bf16[256,4096]{1,0:T(8,128)(2,1)} async-done(((bf16[8,4096]{1,0:T(8,128)(2,1)}), bf16[256,4096]{1,0:T(8,128)(2,1)}) %all-gather.4.cloned.1.call-update) | async-done | bytes 2097168 | tf_op jit(solution)/shard_map/all_gather | solution.py:29
  107.7 2.3 fusion.16
  110.1 3.9 %copy.51 = bf16[1,128,1,4096]{1,2,0,3:T(2,128)(2,1)} copy(bf16[1,128,1,4096]{3,1,2,0:T(8,128)(2,1)S(1)} %fusion.16) | data formatting | bytes 2097152 | tf_op jit(solution)/shard_map/convert_element_type | solution.py:31
  114.6 23.4 %reduce.1 = bf16[4096,128]{1,0:T(8,128)(2,1)S(1)} reduce(bf16[4096,1,1,128]{3,2,1,0:T(2,128)(2,1)} %bitcast.78, bf16[]{:T(256)} %broadcast.42), dimensions={1,2}, to_apply=%bitcast.56.reduce_sub_computation | reduce | bytes 2097154
  139.2 9.9 %all-to-all-start = ((bf16[16,2,16384]{2,1,0:T(2,128)(2,1)}), bf16[16,2,16384]{2,1,0:T(2,128)(2,1)S(1)}, u32[]{:S(2)}, u32[]{:S(2)}) async-start(bf16[16,2,16384]{2,1,0:T(2,128)(2,1)} %reshape.51), calls=%async_computation | async-start | bytes 2097152 | tf_op jit(solution)/shard_map/all_to_all | solution.py:33
  149.2 58.6 %all-gather = bf16[16,4,5120]{2,1,0:T(4,128)(2,1)} all-gather(bf16[1,4,5120]{2,1,0:T(4,128)(2,1)S(1)} %fusion.23), channel_id=1, replica_groups=mesh['fsdp'=32,'seq'=16] {'seq'}, dimensions={0}, use_global_device_ids=true | all-gather | bytes 696320 | tf_op jit(solution)/shard_map/all_gather | solution.py:37
  207.8 2.3 reshape.49
  210.7 1.6 copy.54
  212.3 2.9 copy.55
  215.2 1.5 fusion.25
  216.7 2.3 copy.56
  219.1 1.4 copy.59
  221.7 1.4 copy.52
  224.4 3.4 %copy.81 = bf16[640,8,2,256]{3,1,2,0:T(8,128)(2,1)S(1)} copy(bf16[640,8,2,256]{3,2,1,0:T(2,128)(2,1)} %bitcast.82) | data formatting | bytes 10485760
  229.2 1.4 pad_maximum_fusion
  232.2 1.4 copy.64
  233.6 55.6 %while.11 = (s32[]{:T(128)}, bf16[4,512,2,128]{3,2,1,0:T(2,128)(2,1)}, bf16[4,512,2,128]{3,2,1,0:T(2,128)(2,1)S(1)}, bf16[2112,2,128]{2,0,1:T(8,128)(2,1)S(1)}, ...) while((s32[]{:T(128)}, bf16[4,512,2,128]{3,2,1,0:T(2,128)(2,1)}, ...), condition=%wide.region_5.6_spmd.clone, body=%wide.region_2.5_spmd.clone.sunk | while | flops 1122570368 | bytes 25375472 | solution.py:72
  233.8 7.4 %fusion.38 = (f32[2,512]{1,0:T(2,128)S(1)}, f32[2,512,2112]{1,2,0:T(8,128)}) fusion(pred[2112]{0:T(1024)(128)(4,1)S(1)} %iota_compare_fusion.4, bf16[2112,2,128]{2,0,1:T(8,128)(2,1)S(1)} %get-tuple-element.153, bf16[1,512,2,128]{3,2,1,0:T(2,128)(2,1)S(1)} %constant_dynamic-slice_fusion.2), kind=kOutput, calls=%fused_computation.38.clone.1 | convolution fusion | flops 564463680 | bytes 10000448 | tf_op jit(solution)/shard_map/while/body/eval_jaxpr/sub | solution.py:65
  241.2 5.3 %fusion.39 = bf16[1,512,2,128]{3,1,2,0:T(8,128)(2,1)S(1)} fusion(bf16[2112,2,128]{2,0,1:T(8,128)(2,1)S(1)} %copy-done.4, f32[2,512,2112]{1,2,0:T(8,128)} %get-tuple-element.134, f32[2,512]{1,0:T(2,128)S(1)} %get-tuple-element.135), kind=kOutput, calls=%fused_computation.11.clone.1 | convolution fusion | flops 558104576 | bytes 9998336 | tf_op jit(solution)/shard_map/while/body/eval_jaxpr/hbk,khd->bhd/dot_general | solution.py:68
  247.7 7.4 %fusion.38 = (f32[2,512]{1,0:T(2,128)S(1)}, f32[2,512,2112]{1,2,0:T(8,128)}) fusion(pred[2112]{0:T(1024)(128)(4,1)S(1)} %iota_compare_fusion.4, bf16[2112,2,128]{2,0,1:T(8,128)(2,1)S(1)} %get-tuple-element.153, bf16[1,512,2,128]{3,2,1,0:T(2,128)(2,1)S(1)} %constant_dynamic-slice_fusion.2), kind=kOutput, calls=%fused_computation.38.clone.1 | convolution fusion | flops 564463680 | bytes 10000448 | tf_op jit(solution)/shard_map/while/body/eval_jaxpr/sub | solution.py:65
  255.1 5.3 %fusion.39 = bf16[1,512,2,128]{3,1,2,0:T(8,128)(2,1)S(1)} fusion(bf16[2112,2,128]{2,0,1:T(8,128)(2,1)S(1)} %copy-done.4, f32[2,512,2112]{1,2,0:T(8,128)} %get-tuple-element.134, f32[2,512]{1,0:T(2,128)S(1)} %get-tuple-element.135), kind=kOutput, calls=%fused_computation.11.clone.1 | convolution fusion | flops 558104576 | bytes 9998336 | tf_op jit(solution)/shard_map/while/body/eval_jaxpr/hbk,khd->bhd/dot_general | solution.py:68
  261.6 7.4 %fusion.38 = (f32[2,512]{1,0:T(2,128)S(1)}, f32[2,512,2112]{1,2,0:T(8,128)}) fusion(pred[2112]{0:T(1024)(128)(4,1)S(1)} %iota_compare_fusion.4, bf16[2112,2,128]{2,0,1:T(8,128)(2,1)S(1)} %get-tuple-element.153, bf16[1,512,2,128]{3,2,1,0:T(2,128)(2,1)S(1)} %constant_dynamic-slice_fusion.2), kind=kOutput, calls=%fused_computation.38.clone.1 | convolution fusion | flops 564463680 | bytes 10000448 | tf_op jit(solution)/shard_map/while/body/eval_jaxpr/sub | solution.py:65
  269.0 5.3 %fusion.39 = bf16[1,512,2,128]{3,1,2,0:T(8,128)(2,1)S(1)} fusion(bf16[2112,2,128]{2,0,1:T(8,128)(2,1)S(1)} %copy-done.4, f32[2,512,2112]{1,2,0:T(8,128)} %get-tuple-element.134, f32[2,512]{1,0:T(2,128)S(1)} %get-tuple-element.135), kind=kOutput, calls=%fused_computation.11.clone.1 | convolution fusion | flops 558104576 | bytes 9998336 | tf_op jit(solution)/shard_map/while/body/eval_jaxpr/hbk,khd->bhd/dot_general | solution.py:68
  275.5 7.4 %fusion.38 = (f32[2,512]{1,0:T(2,128)S(1)}, f32[2,512,2112]{1,2,0:T(8,128)}) fusion(pred[2112]{0:T(1024)(128)(4,1)S(1)} %iota_compare_fusion.4, bf16[2112,2,128]{2,0,1:T(8,128)(2,1)S(1)} %get-tuple-element.153, bf16[1,512,2,128]{3,2,1,0:T(2,128)(2,1)S(1)} %constant_dynamic-slice_fusion.2), kind=kOutput, calls=%fused_computation.38.clone.1 | convolution fusion | flops 564463680 | bytes 10000448 | tf_op jit(solution)/shard_map/while/body/eval_jaxpr/sub | solution.py:65
  282.9 5.3 %fusion.39 = bf16[1,512,2,128]{3,1,2,0:T(8,128)(2,1)S(1)} fusion(bf16[2112,2,128]{2,0,1:T(8,128)(2,1)S(1)} %copy-done.4, f32[2,512,2112]{1,2,0:T(8,128)} %get-tuple-element.134, f32[2,512]{1,0:T(2,128)S(1)} %get-tuple-element.135), kind=kOutput, calls=%fused_computation.11.clone.1 | convolution fusion | flops 558104576 | bytes 9998336 | tf_op jit(solution)/shard_map/while/body/eval_jaxpr/hbk,khd->bhd/dot_general | solution.py:68
  289.2 6.6 %reshape.50 = bf16[1,2048,256]{2,0,1:T(2,128)(2,1)S(1)} reshape(bf16[4,512,2,128]{3,2,1,0:T(2,128)(2,1)} %get-tuple-element.37) | data formatting | bytes 2097152 | tf_op jit(solution)/shard_map/reshape | solution.py:72
  295.8 10.6 %reduce.2 = bf16[2048,256]{1,0:T(8,128)(2,1)S(1)} reduce(bf16[2048,1,256]{2,1,0:T(2,128)(2,1)S(1)} %bitcast.80, bf16[]{:T(256)} %broadcast.42), dimensions={1}, to_apply=%bitcast.58.reduce_sub_computation | reduce | bytes 2097154
  306.7 23.5 %all_to_all.51 = bf16[16,2,16384]{2,1,0:T(2,128)(2,1)S(1)} all-to-all(bf16[16,2,16384]{2,1,0:T(2,128)(2,1)S(1)} %reshape.53), channel_id=1, replica_groups=mesh['fsdp'=32,'seq'=16] {'seq'}, dimensions={0} | all-to-all | bytes 2097152 | tf_op jit(solution)/shard_map/all_to_all | solution.py:73
  (63 shorter events, 16.5 us)
Async XLA Ops:
  6.5 101.2 %all-gather.4.cloned.1.call-start = ((), (), s32[]{:S(2)}) async-start(), calls=%async_computation.3 | async-start | bytes 2162688 | tf_op jit(solution)/shard_map/all_gather | solution.py:29
  44.2 180.2 %all-gather.6.cloned.1.call-start = ((), (), s32[]{:S(2)}) async-start(), calls=%async_computation.4 | async-start | bytes 5406720 | tf_op jit(solution)/shard_map/all_gather | solution.py:40
  45.0 1.6 slice-start
  50.3 3.9 %copy-start.5 = (bf16[1,4,5120]{2,1,0:T(4,128)(2,1)S(1)}, bf16[1,4,5120]{2,1,0:T(4,128)(2,1)}, u32[]{:S(2)}) copy-start(bf16[1,4,5120]{2,1,0:T(4,128)(2,1)} %param.9) | copy-start | bytes 122884
  50.3 57.4 %copy-start.6 = (s32[1,128]{1,0:T(1,128)S(1)}, s32[1,128]{1,0:T(1,128)}, u32[]{:S(2)}) copy-start(s32[1,128]{1,0:T(1,128)} %param.12) | copy-start | bytes 1540
  50.3 88.8 %all-to-all-start.1 = ((bf16[1,128,2,4096]{1,2,0,3:T(2,128)(2,1)}), bf16[1,128,2,4096]{1,2,0,3:T(2,128)(2,1)S(1)}, u32[]{:S(2)}, u32[]{:S(2)}) async-start(bf16[1,128,2,4096]{1,2,0,3:T(2,128)(2,1)} %copy.76), calls=%async_computation.1 | async-start | bytes 4194304 | tf_op jit(solution)/shard_map/all_to_all | solution.py:34
  139.2 81.3 %all-to-all-start = ((bf16[16,2,16384]{2,1,0:T(2,128)(2,1)}), bf16[16,2,16384]{2,1,0:T(2,128)(2,1)S(1)}, u32[]{:S(2)}, u32[]{:S(2)}) async-start(bf16[16,2,16384]{2,1,0:T(2,128)(2,1)} %reshape.51), calls=%async_computation | async-start | bytes 2097152 | tf_op jit(solution)/shard_map/all_to_all | solution.py:33
  216.7 2.3 copy-start.1
  224.4 3.4 %copy-start.2 = (bf16[64,5120]{1,0:T(8,128)(2,1)S(1)}, bf16[64,5120]{1,0:T(8,128)(2,1)}, u32[]{:S(2)}) copy-start(bf16[64,5120]{1,0:T(8,128)(2,1)} %reshape.49) | copy-start | bytes 1966084
  229.2 2.9 copy-start
  232.2 1.4 copy-start.3
  233.8 7.4 %copy-start.4 = (bf16[2112,2,128]{2,0,1:T(8,128)(2,1)S(1)}, bf16[2112,2,128]{2,0,1:T(8,128)(2,1)}, u32[]{:S(2)}) copy-start(bf16[2112,2,128]{2,0,1:T(8,128)(2,1)} %get-tuple-element.154) | copy-start | bytes 3244036 | tf_op jit(solution)/shard_map/while
  247.7 7.4 %copy-start.4 = (bf16[2112,2,128]{2,0,1:T(8,128)(2,1)S(1)}, bf16[2112,2,128]{2,0,1:T(8,128)(2,1)}, u32[]{:S(2)}) copy-start(bf16[2112,2,128]{2,0,1:T(8,128)(2,1)} %get-tuple-element.154) | copy-start | bytes 3244036 | tf_op jit(solution)/shard_map/while
  261.6 7.4 %copy-start.4 = (bf16[2112,2,128]{2,0,1:T(8,128)(2,1)S(1)}, bf16[2112,2,128]{2,0,1:T(8,128)(2,1)}, u32[]{:S(2)}) copy-start(bf16[2112,2,128]{2,0,1:T(8,128)(2,1)} %get-tuple-element.154) | copy-start | bytes 3244036 | tf_op jit(solution)/shard_map/while
  275.5 7.4 %copy-start.4 = (bf16[2112,2,128]{2,0,1:T(8,128)(2,1)S(1)}, bf16[2112,2,128]{2,0,1:T(8,128)(2,1)}, u32[]{:S(2)}) copy-start(bf16[2112,2,128]{2,0,1:T(8,128)(2,1)} %get-tuple-element.154) | copy-start | bytes 3244036 | tf_op jit(solution)/shard_map/while
Sparse Core Ops, SparseCore 0:
  44.3 63.3 all-gather.3
  110.9 82.3 all-gather.5
where the time goes:
time: 341 us; the launch traced here: 340 us
  blocking collectives  120 us (35%)
  matrix products  54.2 us (16%)
  waiting for transfers between devices  53.9 us (16%)
  local copies, waits for them, and re-layouts  48.2 us (14%)
  other arithmetic  36 us (11%)
  between operations  14.3 us (4%)
  starting transfers between devices  13.8 us (4%)
    all_gather x1, blocking collectives, shards(): all_rows = lax.all_gather(normed, 'seq', axis=0, tiled=True)  58.6 us
    all_gather x1, waiting for transfers between devices, shards(): codebook = lax.all_gather(codebook_cols, 'fsdp', axis=0, tiled=True)  53.1 us
    all_gather x1, blocking collectives, shards(): codebook_cols = lax.all_gather(pose_table, 'seq', axis=1, tiled=True)  37.7 us
    unnamed x3, other arithmetic  34.1 us
    sub x4, matrix products, attend(): expo = jnp.where(live_keys[None, None, :], jnp.exp(scores - row_max), 0.0)  29.5 us
    all_to_all x1, blocking collectives, shards(): lax.all_to_all(attended, 'seq', split_axis=1, concat_axis=2, tiled=True)  23.5 us
    dot_general x4, matrix products, attend(): jnp.einsum('hbk,khd->bhd', weights, value_rows, preferred_element_type=jn...  21.3 us
    unnamed x24, local copies, waits for them, and re-layouts  16.6 us
  transfers between devices with their start and end apart: 4, of which 1 were waited for; matrix products, arithmetic and copies ran while one was open for 15% of the time, Pallas kernels for 0%

commit v1 on v0

--- a/solution.py
+++ b/solution.py
@@ -70,7 +70,16 @@
 
     query_blocks = query_heads.reshape(block_count, block_rows, heads_here, HD)
     attended = lax.map(attend, query_blocks).reshape(1, video_len, head_width)
-    return lax.all_to_all(attended, "seq", split_axis=1, concat_axis=2, tiled=True)
+    place_cycles_in = lambda array_in, axis_tag: jnp.concatenate(
+        lax.all_to_all(
+            jnp.stack(jnp.split(array_in, lax.axis_size(axis_tag), 1), 0),
+            axis_name=axis_tag,
+            split_axis=0,
+            concat_axis=0,
+        ),
+        2,
+    )
+    return place_cycles_in(attended, "seq")
 
 
 def solution(mesh):

time: 341 us -> 324 us (0.950)
  the two profiles are of different devices: /device:TPU:4 before, /device:TPU:2 now
where the time goes in v1:
time: 324 us; the launch traced here: 323 us
  blocking collectives  120 us (37%)
  matrix products  54.2 us (17%)
  waiting for transfers between devices  54 us (17%)
  local copies, waits for them, and re-layouts  41.2 us (13%)
  other arithmetic  25.4 us (8%)
  between operations  14.4 us (4%)
  starting transfers between devices  13.2 us (4%)
    all_gather x1, blocking collectives, shards(): all_rows = lax.all_gather(normed, 'seq', axis=0, tiled=True)  58.9 us
    all_gather x1, waiting for transfers between devices, shards(): codebook = lax.all_gather(codebook_cols, 'fsdp', axis=0, tiled=True)  53.3 us
    all_gather x1, blocking collectives, shards(): codebook_cols = lax.all_gather(pose_table, 'seq', axis=1, tiled=True)  37.7 us
    sub x4, matrix products, attend(): expo = jnp.where(live_keys[None, None, :], jnp.exp(scores - row_max), 0.0)  29.5 us
    all_to_all x1, blocking collectives, shards(): lax.all_to_all(jnp.stack(jnp.split(array_in, lax.axis_size(axis_tag), 1),...  23.7 us
    unnamed x2, other arithmetic  23.5 us
    dot_general x4, matrix products, attend(): jnp.einsum('hbk,khd->bhd', weights, value_rows, preferred_element_type=jn...  21.3 us
    unnamed x36, local copies, waits for them, and re-layouts  15.2 us
  transfers between devices with their start and end apart: 4, of which 1 were waited for; matrix products, arithmetic and copies ran while one was open for 16% of the time, Pallas kernels for 0%

profile of v1, /device:TPU:2, one launch (start us, length us, event | category | flops | bytes accessed | tf_op | source)
XLA Modules:
  0.0 322.8 jit_solution(14775819270442076817)
XLA Ops:
  6.5 37.7 %all_gather.12 = bf16[8,4096]{1,0:T(8,128)(2,1)} all-gather(bf16[8,256]{1,0:T(8,128)(2,1)} %param.11), channel_id=1, replica_groups=mesh['fsdp'=32,'seq'=16] {'seq'}, dimensions={1}, use_global_device_ids=true | all-gather | bytes 69632 | tf_op jit(solution)/shard_map/all_gather | solution.py:28
  45.8 3.8 %copy.88 = bf16[1,128,2,4096]{1,2,0,3:T(2,128)(2,1)} copy(bf16[1,128,2,4096]{3,1,2,0:T(8,128)(2,1)S(1)} %slice-done) | data formatting | bytes 4194304
  49.6 3.8 %all-to-all-start.1 = ((bf16[1,128,2,4096]{1,2,0,3:T(2,128)(2,1)}), bf16[1,128,2,4096]{1,2,0,3:T(2,128)(2,1)S(1)}, u32[]{:S(2)}, u32[]{:S(2)}) async-start(bf16[1,128,2,4096]{1,2,0,3:T(2,128)(2,1)} %copy.88), calls=%async_computation.1 | async-start | bytes 4194304 | tf_op jit(solution)/shard_map/all_to_all | solution.py:34
  53.9 53.3 %all-gather.4.cloned.1.call-done = bf16[256,4096]{1,0:T(8,128)(2,1)} async-done(((bf16[8,4096]{1,0:T(8,128)(2,1)}), bf16[256,4096]{1,0:T(8,128)(2,1)}) %all-gather.4.cloned.1.call-update) | async-done | bytes 2097168 | tf_op jit(solution)/shard_map/all_gather | solution.py:29
  107.2 2.3 fusion.16
  109.5 3.9 %copy.65 = bf16[1,128,1,4096]{1,2,0,3:T(2,128)(2,1)} copy(bf16[1,128,1,4096]{3,1,2,0:T(8,128)(2,1)S(1)} %fusion.16) | data formatting | bytes 2097152 | tf_op jit(solution)/shard_map/convert_element_type | solution.py:31
  113.9 23.4 %reduce.1 = bf16[4096,128]{1,0:T(8,128)(2,1)S(1)} reduce(bf16[4096,1,1,128]{3,2,1,0:T(2,128)(2,1)} %bitcast.137, bf16[]{:T(256)} %broadcast.42), dimensions={1,2}, to_apply=%bitcast.118.reduce_sub_computation | reduce | bytes 2097154
  138.5 9.3 %all-to-all-start = ((bf16[16,2,16384]{2,1,0:T(2,128)(2,1)}), bf16[16,2,16384]{2,1,0:T(2,128)(2,1)S(1)}, u32[]{:S(2)}, u32[]{:S(2)}) async-start(bf16[16,2,16384]{2,1,0:T(2,128)(2,1)} %reshape.58), calls=%async_computation | async-start | bytes 2097152 | tf_op jit(solution)/shard_map/all_to_all | solution.py:33
  148.0 58.9 %all-gather = bf16[16,4,5120]{2,1,0:T(4,128)(2,1)} all-gather(bf16[1,4,5120]{2,1,0:T(4,128)(2,1)S(1)} %fusion.39), channel_id=1, replica_groups=mesh['fsdp'=32,'seq'=16] {'seq'}, dimensions={0}, use_global_device_ids=true | all-gather | bytes 696320 | tf_op jit(solution)/shard_map/all_gather | solution.py:37
  206.9 2.3 reshape.57
  209.8 1.6 copy.68
  211.4 2.9 copy.69
  214.3 1.5 fusion.41
  215.8 2.3 copy.70
  218.1 1.4 copy.73
  220.8 1.4 copy.66
  222.1 1.3 reshape.50
  223.5 3.4 %copy.93 = bf16[640,8,2,256]{3,1,2,0:T(8,128)(2,1)S(1)} copy(bf16[640,8,2,256]{3,2,1,0:T(2,128)(2,1)} %bitcast.140) | data formatting | bytes 10485760
  228.3 1.4 pad_maximum_fusion
  229.7 1.3 copy.77
  231.3 1.4 copy.78
  232.7 55.7 %while.11 = (s32[]{:T(128)}, bf16[4,512,2,128]{3,2,1,0:T(2,128)(2,1)}, bf16[4,512,2,128]{3,2,1,0:T(2,128)(2,1)S(1)}, bf16[2112,2,128]{2,0,1:T(8,128)(2,1)S(1)}, ...) while((s32[]{:T(128)}, bf16[4,512,2,128]{3,2,1,0:T(2,128)(2,1)}, ...), condition=%wide.region_5.6_spmd.clone, body=%wide.region_2.5_spmd.clone.sunk | while | flops 1122570368 | bytes 25375472 | solution.py:72
  232.9 7.4 %fusion.54 = (f32[2,512]{1,0:T(2,128)S(1)}, f32[2,512,2112]{1,2,0:T(8,128)}) fusion(pred[2112]{0:T(1024)(128)(4,1)S(1)} %iota_compare_fusion.4, bf16[2112,2,128]{2,0,1:T(8,128)(2,1)S(1)} %get-tuple-element.153, bf16[1,512,2,128]{3,2,1,0:T(2,128)(2,1)S(1)} %constant_dynamic-slice_fusion.2), kind=kOutput, calls=%fused_computation.70.clone.1 | convolution fusion | flops 564463680 | bytes 10000448 | tf_op jit(solution)/shard_map/while/body/eval_jaxpr/sub | solution.py:65
  240.3 5.3 %fusion.55 = bf16[1,512,2,128]{3,1,2,0:T(8,128)(2,1)S(1)} fusion(bf16[2112,2,128]{2,0,1:T(8,128)(2,1)S(1)} %copy-done.4, f32[2,512,2112]{1,2,0:T(8,128)} %get-tuple-element.134, f32[2,512]{1,0:T(2,128)S(1)} %get-tuple-element.135), kind=kOutput, calls=%fused_computation.11.clone.1 | convolution fusion | flops 558104576 | bytes 9998336 | tf_op jit(solution)/shard_map/while/body/eval_jaxpr/hbk,khd->bhd/dot_general | solution.py:68
  246.8 7.4 %fusion.54 = (f32[2,512]{1,0:T(2,128)S(1)}, f32[2,512,2112]{1,2,0:T(8,128)}) fusion(pred[2112]{0:T(1024)(128)(4,1)S(1)} %iota_compare_fusion.4, bf16[2112,2,128]{2,0,1:T(8,128)(2,1)S(1)} %get-tuple-element.153, bf16[1,512,2,128]{3,2,1,0:T(2,128)(2,1)S(1)} %constant_dynamic-slice_fusion.2), kind=kOutput, calls=%fused_computation.70.clone.1 | convolution fusion | flops 564463680 | bytes 10000448 | tf_op jit(solution)/shard_map/while/body/eval_jaxpr/sub | solution.py:65
  254.2 5.3 %fusion.55 = bf16[1,512,2,128]{3,1,2,0:T(8,128)(2,1)S(1)} fusion(bf16[2112,2,128]{2,0,1:T(8,128)(2,1)S(1)} %copy-done.4, f32[2,512,2112]{1,2,0:T(8,128)} %get-tuple-element.134, f32[2,512]{1,0:T(2,128)S(1)} %get-tuple-element.135), kind=kOutput, calls=%fused_computation.11.clone.1 | convolution fusion | flops 558104576 | bytes 9998336 | tf_op jit(solution)/shard_map/while/body/eval_jaxpr/hbk,khd->bhd/dot_general | solution.py:68
  260.7 7.4 %fusion.54 = (f32[2,512]{1,0:T(2,128)S(1)}, f32[2,512,2112]{1,2,0:T(8,128)}) fusion(pred[2112]{0:T(1024)(128)(4,1)S(1)} %iota_compare_fusion.4, bf16[2112,2,128]{2,0,1:T(8,128)(2,1)S(1)} %get-tuple-element.153, bf16[1,512,2,128]{3,2,1,0:T(2,128)(2,1)S(1)} %constant_dynamic-slice_fusion.2), kind=kOutput, calls=%fused_computation.70.clone.1 | convolution fusion | flops 564463680 | bytes 10000448 | tf_op jit(solution)/shard_map/while/body/eval_jaxpr/sub | solution.py:65
  268.1 5.3 %fusion.55 = bf16[1,512,2,128]{3,1,2,0:T(8,128)(2,1)S(1)} fusion(bf16[2112,2,128]{2,0,1:T(8,128)(2,1)S(1)} %copy-done.4, f32[2,512,2112]{1,2,0:T(8,128)} %get-tuple-element.134, f32[2,512]{1,0:T(2,128)S(1)} %get-tuple-element.135), kind=kOutput, calls=%fused_computation.11.clone.1 | convolution fusion | flops 558104576 | bytes 9998336 | tf_op jit(solution)/shard_map/while/body/eval_jaxpr/hbk,khd->bhd/dot_general | solution.py:68
  274.6 7.4 %fusion.54 = (f32[2,512]{1,0:T(2,128)S(1)}, f32[2,512,2112]{1,2,0:T(8,128)}) fusion(pred[2112]{0:T(1024)(128)(4,1)S(1)} %iota_compare_fusion.4, bf16[2112,2,128]{2,0,1:T(8,128)(2,1)S(1)} %get-tuple-element.153, bf16[1,512,2,128]{3,2,1,0:T(2,128)(2,1)S(1)} %constant_dynamic-slice_fusion.2), kind=kOutput, calls=%fused_computation.70.clone.1 | convolution fusion | flops 564463680 | bytes 10000448 | tf_op jit(solution)/shard_map/while/body/eval_jaxpr/sub | solution.py:65
  282.0 5.3 %fusion.55 = bf16[1,512,2,128]{3,1,2,0:T(8,128)(2,1)S(1)} fusion(bf16[2112,2,128]{2,0,1:T(8,128)(2,1)S(1)} %copy-done.4, f32[2,512,2112]{1,2,0:T(8,128)} %get-tuple-element.134, f32[2,512]{1,0:T(2,128)S(1)} %get-tuple-element.135), kind=kOutput, calls=%fused_computation.11.clone.1 | convolution fusion | flops 558104576 | bytes 9998336 | tf_op jit(solution)/shard_map/while/body/eval_jaxpr/hbk,khd->bhd/dot_general | solution.py:68
  288.3 1.7 reshape.53
  290.3 23.7 %all_to_all.38 = bf16[16,1,128,256]{3,2,1,0:T(8,128)(2,1)S(1)} all-to-all(bf16[16,1,128,256]{3,2,1,0:T(8,128)(2,1)S(1)} %fusion.22), channel_id=1, replica_groups=mesh['fsdp'=32,'seq'=16] {'seq'}, dimensions={0} | all-to-all | bytes 2097152 | tf_op jit(solution)/shard_map/all_to_all | solution.py:74
  (75 shorter events, 13.2 us)
Async XLA Ops:
  6.5 100.6 %all-gather.4.cloned.1.call-start = ((), (), s32[]{:S(2)}) async-start(), calls=%async_computation.3 | async-start | bytes 2162688 | tf_op jit(solution)/shard_map/all_gather | solution.py:29
  44.2 1.6 slice-start
  44.2 179.3 %all-gather.6.cloned.1.call-start = ((), (), s32[]{:S(2)}) async-start(), calls=%async_computation.4 | async-start | bytes 5406720 | tf_op jit(solution)/shard_map/all_gather | solution.py:40
  49.6 3.9 %copy-start.5 = (bf16[1,4,5120]{2,1,0:T(4,128)(2,1)S(1)}, bf16[1,4,5120]{2,1,0:T(4,128)(2,1)}, u32[]{:S(2)}) copy-start(bf16[1,4,5120]{2,1,0:T(4,128)(2,1)} %param.9) | copy-start | bytes 122884
  49.6 57.5 %copy-start.6 = (s32[1,128]{1,0:T(1,128)S(1)}, s32[1,128]{1,0:T(1,128)}, u32[]{:S(2)}) copy-start(s32[1,128]{1,0:T(1,128)} %param.12) | copy-start | bytes 1540
  49.6 88.9 %all-to-all-start.1 = ((bf16[1,128,2,4096]{1,2,0,3:T(2,128)(2,1)}), bf16[1,128,2,4096]{1,2,0,3:T(2,128)(2,1)S(1)}, u32[]{:S(2)}, u32[]{:S(2)}) async-start(bf16[1,128,2,4096]{1,2,0,3:T(2,128)(2,1)} %copy.88), calls=%async_computation.1 | async-start | bytes 4194304 | tf_op jit(solution)/shard_map/all_to_all | solution.py:34
  138.5 81.0 %all-to-all-start = ((bf16[16,2,16384]{2,1,0:T(2,128)(2,1)}), bf16[16,2,16384]{2,1,0:T(2,128)(2,1)S(1)}, u32[]{:S(2)}, u32[]{:S(2)}) async-start(bf16[16,2,16384]{2,1,0:T(2,128)(2,1)} %reshape.58), calls=%async_computation | async-start | bytes 2097152 | tf_op jit(solution)/shard_map/all_to_all | solution.py:33
  215.8 2.4 copy-start.1
  223.5 3.4 %copy-start.2 = (bf16[64,5120]{1,0:T(8,128)(2,1)S(1)}, bf16[64,5120]{1,0:T(8,128)(2,1)}, u32[]{:S(2)}) copy-start(bf16[64,5120]{1,0:T(8,128)(2,1)} %reshape.57) | copy-start | bytes 1966084
  228.2 2.9 copy-start
  231.2 1.4 copy-start.3
  232.9 7.4 %copy-start.4 = (bf16[2112,2,128]{2,0,1:T(8,128)(2,1)S(1)}, bf16[2112,2,128]{2,0,1:T(8,128)(2,1)}, u32[]{:S(2)}) copy-start(bf16[2112,2,128]{2,0,1:T(8,128)(2,1)} %get-tuple-element.154) | copy-start | bytes 3244036 | tf_op jit(solution)/shard_map/while
  246.8 7.4 %copy-start.4 = (bf16[2112,2,128]{2,0,1:T(8,128)(2,1)S(1)}, bf16[2112,2,128]{2,0,1:T(8,128)(2,1)}, u32[]{:S(2)}) copy-start(bf16[2112,2,128]{2,0,1:T(8,128)(2,1)} %get-tuple-element.154) | copy-start | bytes 3244036 | tf_op jit(solution)/shard_map/while
  260.7 7.4 %copy-start.4 = (bf16[2112,2,128]{2,0,1:T(8,128)(2,1)S(1)}, bf16[2112,2,128]{2,0,1:T(8,128)(2,1)}, u32[]{:S(2)}) copy-start(bf16[2112,2,128]{2,0,1:T(8,128)(2,1)} %get-tuple-element.154) | copy-start | bytes 3244036 | tf_op jit(solution)/shard_map/while
  274.6 7.4 %copy-start.4 = (bf16[2112,2,128]{2,0,1:T(8,128)(2,1)S(1)}, bf16[2112,2,128]{2,0,1:T(8,128)(2,1)}, u32[]{:S(2)}) copy-start(bf16[2112,2,128]{2,0,1:T(8,128)(2,1)} %get-tuple-element.154) | copy-start | bytes 3244036 | tf_op jit(solution)/shard_map/while
Sparse Core Ops, SparseCore 0:
  44.3 62.7 all-gather.3
  110.3 82.6 all-gather.5
